TPU v7x, 128 devices: a whole 4x4x4 slice. The times are simulated.
128 devices in a mesh: ag: 16 (over y, z_lo, core), tm: 8 (over z_hi, x).
Axes of the slice: x: 4, y: 4, z: 4 (z_hi: 2, z_lo: 2; z = z_hi * 2 + z_lo), core: 2. Of those that a mesh axis runs over, the one named last changes fastest.
Arguments:
- tokens: bfloat16 [1, 256, 128, 1024], P(None, 'ag', 'tm'), may hold values from -6 to 6
- cotangent: bfloat16 [1, 256, 128, 1024], P(None, 'ag', 'tm'), may hold values from -6 to 6
- observed: int32 [1, 256, 128], replicated, may hold values from 0 to 1, as said below
- time_qkv: bfloat16 [1024, 3072], replicated, may hold values from -12 to 12
- time_out: bfloat16 [1024, 1024], replicated, may hold values from -0.1875 to 0.1875
- agent_qkv: bfloat16 [1024, 3072], replicated, may hold values from -12 to 12
- agent_out: bfloat16 [1024, 1024], replicated, may hold values from -0.1875 to 0.1875
Outputs:
- grad_tokens: bfloat16 [1, 256, 128, 1024], P(None, 'ag', 'tm')
- grad_time_qkv: float32 [1024, 3072], P(('ag', 'tm'))
- grad_time_out: float32 [1024, 1024], P(('ag', 'tm'))
- grad_agent_qkv: float32 [1024, 3072], P(('ag', 'tm'))
- grad_agent_out: float32 [1024, 1024], P(('ag', 'tm'))
Inputs may be any that keep to these rules, and one draw needn't show every extreme that they name: 1 marks an observed step of a present agent; each scene's present agents come first, each observed over one run of steps.
All inputs are finite; a program needn't handle non-finite values.
Results may differ from a plain program's by a relative error of at most 0.012.
Values may be sent and summed in bfloat16 or wider, within the bound.
A program may use at most 192 MiB of HBM per device.

v0:
```python
import functools

import jax
import jax.numpy as jnp
from jax import lax
from jax.experimental import pallas as pl
from jax.experimental.pallas import tpu as pltpu
from jax.sharding import PartitionSpec as P

D = 1024
H = 16
HD = 64
STEPS = 128
epsilon = 1e-06
masked_score = -1e30

MESH = pl.DeviceIdType.MESH
BF = jnp.bfloat16
F32 = jnp.float32
NT = (((1,), (1,)), ((), ()))
TN = (((0,), (0,)), ((), ()))

STREAMS = ((0, 1408, "xyz"), (1408, 2816, "yzx"), (2816, 4096, "zyx"))


def matmul(left, right, dims=(((1,), (0,)), ((), ()))):
    return lax.dot_general(left, right, dims, preferred_element_type=F32)


class Place:
    def __init__(self):
        self.ag = lax.axis_index("ag")
        self.tm = lax.axis_index("tm")
        self.y = self.ag // 4
        self.zlo = (self.ag // 2) % 2
        self.core = self.ag % 2
        self.zhi = self.tm // 4
        self.x = self.tm % 4
        self.z = self.zhi * 2 + self.zlo

    def at(self, axis):
        return {"x": self.x, "y": self.y, "z": self.z}[axis]

    def ring(self, axis, step):
        if axis == "x":
            return (self.ag, self.zhi * 4 + (self.x + step) % 4)
        if axis == "y":
            return (((self.y + step) % 4) * 4 + self.ag % 4, self.tm)
        z = (self.z + step) % 4
        return (self.y * 4 + (z % 2) * 2 + self.core, (z // 2) * 4 + self.x)

    def twin(self):
        return (self.ag + 1 - 2 * self.core, self.tm)


def remote(src, dst, send, recv, device):
    return pltpu.make_async_remote_copy(
        src_ref=src, dst_ref=dst, send_sem=send, recv_sem=recv, device_id=device, device_id_type=MESH
    )


def greet(devices):
    barrier = pltpu.get_barrier_semaphore()
    for device in devices:
        pl.semaphore_signal(barrier, inc=1, device_id=device, device_id_type=MESH)
    pl.semaphore_wait(barrier, len(devices))


def selector(core, x_first):
    at = lax.broadcasted_iota(jnp.int32, (128, 256), 0)
    row = lax.broadcasted_iota(jnp.int32, (128, 256), 1)
    high, low = at // 32, (at // 8) % 4
    x, z = (high, low) if x_first else (low, high)
    wanted = (z % 2) * 128 + core * 64 + (z // 2) * 32 + x * 8 + at % 8
    return jnp.where(row == wanted, 1.0, 0.0).astype(BF)


class Twin:
    def __init__(self, place, send, recv):
        self.place, self.send, self.recv = place, send, recv

    def copy(self, slot, ref, cols=None):
        cols = slice(None) if cols is None else cols
        return remote(
            ref.at[0:256, cols], ref.at[256:512, cols], self.send.at[slot], self.recv.at[slot], self.place.twin()
        )

    def copy_rows(self, slot, ref):
        return remote(ref.at[0:2], ref.at[2:4], self.send.at[slot], self.recv.at[slot], self.place.twin())


class Scatter:
    def __init__(self, place, block, bufs, send, recv):
        self.place = place
        self.block, (self.own, self.r1, self.s2, self.r2, self.s3, self.r3) = block, bufs
        self.send, self.recv = send, recv

    def copy(self, stream, phase, step):
        lo, hi, axes = STREAMS[stream]
        cols = slice(lo, hi)
        axis = axes[phase]
        to = (self.place.at(axis) + step) % 4
        slot = step - 1
        if phase == 0:
            src, dst = self.block(stream, slot), self.r1.at[slot, :, cols]
        elif phase == 1:
            src = self.s2.at[pl.ds(pl.multiple_of(to * 32, 32), 32), cols]
            dst = self.r2.at[slot, :, cols]
        else:
            src = self.s3.at[pl.ds(pl.multiple_of(to * 8, 8), 8), cols]
            dst = self.r3.at[slot, :, cols]
        return remote(
            src,
            dst,
            self.send.at[stream, phase, slot],
            self.recv.at[stream, phase, slot],
            self.place.ring(axis, step),
        )

    def product(self, stream, ut, ut_mixed, gm, g, block):
        lo, hi, _ = STREAMS[stream]
        rows = pl.ds(pl.multiple_of(block * 128, 128), 128)
        if stream < 2:
            return [(lo, hi, matmul(ut[stream, rows, :], gm[:, lo:hi]))]
        return [
            (lo, 3072, matmul(ut[2, rows, :], gm[:, lo:3072])),
            (3072, 4096, matmul(ut_mixed[rows, :], g[...].reshape(512, D))),
        ]

    def start(self, stream, ut, ut_mixed, gm, g):
        first, _, axes = STREAMS[stream]
        at = self.place.at(axes[0])

        def one(step, carry):
            for lo, hi, part in self.product(stream, ut, ut_mixed, gm, g, (at + step) % 4):
                self.block(stream, step - 1)[:, lo - first : hi - first] = part.astype(BF)
            self.copy(stream, 0, step).start()
            return carry

        lax.fori_loop(1, 4, one, 0)
        for lo, hi, part in self.product(stream, ut, ut_mixed, gm, g, at):
            self.own[:, lo:hi] = part

    def second(self, stream):
        lo, hi, _ = STREAMS[stream]
        for step in (1, 2, 3):
            self.copy(stream, 0, step).wait_recv()

        def one(q, carry):
            rows = pl.ds(pl.multiple_of(q * 32, 32), 32)
            total = self.own[rows, lo:hi]
            for slot in range(3):
                total = total + self.r1[slot, rows, lo:hi].astype(F32)
            self.own[rows, lo:hi] = total
            self.s2[rows, lo:hi] = total.astype(BF)
            return carry

        lax.fori_loop(0, 4, one, 0)
        for step in (1, 2, 3):
            self.copy(stream, 1, step).start()

    def third(self, stream):
        lo, hi, axes = STREAMS[stream]
        for step in (1, 2, 3):
            self.copy(stream, 1, step).wait_recv()
        total = self.own[pl.ds(pl.multiple_of(self.place.at(axes[1]) * 32, 32), 32), lo:hi]
        for slot in range(3):
            total = total + self.r2[slot, :, lo:hi].astype(F32)
        self.s3[:, lo:hi] = total
        for step in (1, 2, 3):
            self.copy(stream, 2, step).start()

    def last(self, stream, qkv_ref, out_ref):
        lo, hi, axes = STREAMS[stream]
        for step in (1, 2, 3):
            self.copy(stream, 2, step).wait_recv()
        total = self.s3[pl.ds(pl.multiple_of(self.place.at(axes[2]) * 8, 8), 8), lo:hi]
        for slot in range(3):
            total = total + self.r3[slot, :, lo:hi]
        top = min(hi, 3072)
        qkv_ref[:, lo:top] = total[:, : top - lo]
        if hi > 3072:
            out_ref[...] = total[:, 3072 - lo :]

    def drain(self):
        for stream in range(3):
            for phase in range(3):
                for step in (1, 2, 3):
                    self.copy(stream, phase, step).wait_send()


def scatter_bufs():
    return [
        pltpu.VMEM((128, 4096), F32),
        pltpu.VMEM((3, 128, 4096), BF),
        pltpu.VMEM((128, 4096), BF),
        pltpu.VMEM((3, 32, 4096), BF),
        pltpu.VMEM((32, 4096), F32),
        pltpu.VMEM((3, 8, 4096), F32),
    ]


def transposed(place, unit, mixed, ut, ut_mixed):
    sel_x = selector(place.core, True)
    sel_z = selector(place.core, False)
    for y in range(4):
        cols = slice(y * 256, y * 256 + 256)
        part = matmul(sel_x, unit[:, cols], NT).astype(BF)
        for x in range(4):
            ut[0, x * 128 + y * 32 : x * 128 + y * 32 + 32, :] = part[x * 32 : x * 32 + 32]
        part = matmul(sel_z, unit[:, cols], NT).astype(BF)
        ut[1, y * 128 : y * 128 + 128, :] = part
        for z in range(4):
            ut[2, z * 128 + y * 32 : z * 128 + y * 32 + 32, :] = part[z * 32 : z * 32 + 32]
        part = matmul(sel_z, mixed[:, cols], NT).astype(BF)
        for z in range(4):
            ut_mixed[z * 128 + y * 32 : z * 128 + y * 32 + 32, :] = part[z * 32 : z * 32 + 32]


def normal(x_ref):
    x = x_ref[...].reshape(256, D).astype(F32)
    inverse = lax.rsqrt(jnp.mean(x * x, axis=-1, keepdims=True) + epsilon)
    return x * inverse, inverse


def span(start, size):
    return pl.ds(pl.multiple_of(start * size, size), size)


def project(x_ref, unit, w, merged):
    unit[0:256, :] = normal(x_ref)[0].astype(BF)

    def one(n, carry):
        cols = span(n, 512)
        merged[:, cols] = matmul(unit[0:256, :], w[:, cols]).astype(BF)
        return carry

    lax.fori_loop(0, 6, one, 0)


def halves():
    lane = lax.broadcasted_iota(jnp.int32, (1, 128), 1)
    low = jnp.where(lane < HD, 1.0, 0.0)
    return low.astype(BF), (1.0 - low).astype(BF)


def pair_parts(merged, rows, pair):
    q = merged[rows, span(pair, 128)] * BF(HD**-0.5)
    k = merged[rows, pl.ds(pl.multiple_of(D + pair * 128, 128), 128)]
    v = merged[rows, pl.ds(pl.multiple_of(2 * D + pair * 128, 128), 128)]
    return q, k, v


def prob_of(q, k, bias):
    scores = matmul(q, k, NT) + bias
    shifted = jnp.exp(scores - jnp.max(scores, axis=-1, keepdims=True))
    return shifted * (1.0 / jnp.sum(shifted, axis=-1, keepdims=True))


def attend(merged, mixed, rows, bias_ref):
    def one(pair, carry):
        q, k, v = pair_parts(merged, rows, pair)
        total = None
        for half in halves():
            part = matmul(prob_of(q * half, k, bias_ref[...]).astype(BF), v * half)
            total = part if total is None else total + part
        mixed[rows, span(pair, 128)] = total.astype(BF)
        return carry

    lax.fori_loop(0, H // 2, one, 0)


def attend_back(merged, gmix, mixed, gm, rows, bias_ref):
    def one(pair, carry):
        q, k, v = pair_parts(merged, rows, pair)
        go = gmix[rows, span(pair, 128)]
        sums = [None] * 4
        for half in halves():
            prob = prob_of(q * half, k, bias_ref[...])
            rounded = prob.astype(BF)
            go_half = go * half
            gp = matmul(go_half, v, NT)
            gs = (prob * (gp - jnp.sum(gp * prob, axis=-1, keepdims=True))).astype(BF)
            parts = [
                matmul(gs, k * half),
                matmul(gs, q * half, TN),
                matmul(rounded, go_half, TN),
                None if mixed is None else matmul(rounded, v * half),
            ]
            sums = [p if s is None else s + p for s, p in zip(sums, parts)]
        gm[rows, span(pair, 128)] = (sums[0] * HD**-0.5).astype(BF)
        gm[rows, pl.ds(pl.multiple_of(D + pair * 128, 128), 128)] = sums[1].astype(BF)
        gm[rows, pl.ds(pl.multiple_of(2 * D + pair * 128, 128), 128)] = sums[2].astype(BF)
        if mixed is not None:
            mixed[rows, span(pair, 128)] = sums[3].astype(BF)
        return carry

    lax.fori_loop(0, H // 2, one, 0)


def add_residual(x_ref, mixed, w, out_ref, shape):
    for n in range(2):
        cols = slice(n * 512, n * 512 + 512)
        x = x_ref[..., cols].reshape(256, 512).astype(F32)
        out = x + matmul(mixed[0:256, :], w[:, cols])
        out_ref[..., cols] = out.astype(BF).reshape(shape + (512,))


def grad_of_mixed(g, w, gmix):
    def one(n, carry):
        rows = span(n, 256)
        gmix[:, rows] = matmul(g[...].reshape(256, D), w[rows, :], NT).astype(BF)
        return carry

    lax.fori_loop(0, 4, one, 0)


def grad_of_input(x_ref, g, gm, w, gu, out_ref, shape):
    def one(n, carry):
        rows = span(n, 256)
        gu[:, rows] = matmul(gm[0:256, :], w[rows, :], NT)
        return carry

    lax.fori_loop(0, 4, one, 0)
    normed, inverse = normal(x_ref)
    grad_unit = gu[...]
    rows = inverse * (grad_unit - normed * jnp.mean(grad_unit * normed, axis=-1, keepdims=True))
    out_ref[...] = (g[...].reshape(256, D).astype(F32) + rows).astype(BF).reshape(shape + (D,))


def swap_rows(src, dst):
    at = lax.broadcasted_iota(jnp.int32, (256, 256), 0)
    row = lax.broadcasted_iota(jnp.int32, (256, 256), 1)
    swap = jnp.where(row == (at % 16) * 16 + at // 16, 1.0, 0.0).astype(BF)
    for n in range(2):
        cols = slice(n * 512, n * 512 + 512)
        out = matmul(swap, src[..., cols].reshape(256, 512)).astype(BF)
        dst[..., cols] = out.reshape(dst.shape[:-1] + (512,))


class Swap:
    def __init__(self, place, axis, send, recv, source, target):
        self.place, self.axis, self.send, self.recv = place, axis, send, recv
        self.source, self.target = source, target
        self.size = 8 if axis == "tm" else 16
        self.me = place.tm if axis == "tm" else place.ag

    def copy(self, step):
        to = (self.me + step) % self.size
        device = (self.place.ag, to) if self.axis == "tm" else (to, self.place.tm)
        return remote(self.source(to), self.target(self.me), self.send.at[step], self.recv.at[step], device)

    def local(self):
        return pltpu.make_async_copy(self.source(self.me), self.target(self.me), self.recv.at[0])

    def start(self):
        def one(step, carry):
            self.copy(step).start()
            return carry

        lax.fori_loop(1, self.size, one, 0)
        self.local().start()

    def wait(self):
        def one(step, carry):
            self.copy(step).wait_recv()
            return carry

        lax.fori_loop(1, self.size, one, 0)
        self.local().wait()

    def drain(self):
        def one(step, carry):
            self.copy(step).wait_send()
            return carry

        lax.fori_loop(1, self.size, one, 0)


def block_kernel(
    tokens, cotangent, observed, time_qkv, time_out, agent_qkv, agent_out,
    grad_tokens, tq_ref, to_ref, aq_ref, ao_ref,
    w_tq, w_to, w_aq, w_ao,
    x_time, made, home, turned, x_agent, cot, back,
    merged_t, merged_a, gmix, gu, bias_t, bias_a,
    units, gms, mixeds, g_time, g_agent, ut, ut_mixed,
    *rest,
):
    grad_a = rest[0]
    bufs = (rest[1:7], rest[7:13])
    load, swap_send, swap_recv, twin_send, twin_recv, sc_send, sc_recv = rest[13:]
    place = Place()
    loads = [
        pltpu.make_async_copy(src, dst, load.at[i])
        for i, (src, dst) in enumerate(
            (
                (cotangent, cot),
                (time_qkv, w_tq),
                (time_out, w_to),
                (agent_out, w_ao),
                (agent_qkv, w_aq),
            )
        )
    ]
    for copy in loads:
        copy.start()
    far = [
        (place.y * 4 + (1 - place.zlo) * 2 + place.core, (1 - place.zhi) * 4 + place.x),
    ]
    greet(
        [((place.ag + step) % 16, place.tm) for step in range(1, 16)]
        + [(place.ag, (place.tm + step) % 8) for step in range(1, 8)]
        + far
    )

    def swap(slot, axis, source, target):
        return Swap(place, axis, swap_send.at[slot], swap_recv.at[slot], source, target)

    def two(ref):
        return lambda i: ref.at[pl.ds(i * 2, 2)]

    def sixteen(ref):
        return lambda i: ref.at[0:2, span(i, 16), :]

    def rows16(ref):
        return lambda i: ref.at[span(i, 16), :]

    tokens_in = swap(0, "tm", two(tokens), sixteen(x_time))
    cot_in = swap(1, "ag", rows16(turned), rows16(g_agent))
    first_home = swap(2, "tm", sixteen(made), two(home))
    first_agent = swap(3, "ag", rows16(turned), rows16(x_agent))
    back_home = swap(4, "ag", rows16(cot), rows16(back))
    back_time = swap(5, "tm", two(home), sixteen(g_time))
    tokens_out = swap(6, "tm", sixteen(made), two(grad_tokens))
    twins = [Twin(place, twin_send.at[s], twin_recv.at[s]) for s in range(2)]

    def block_a(stream, slot):
        lo, hi, _ = STREAMS[stream]
        return grad_a.at[slot, :, lo:hi]

    def block_t(stream, slot):
        lo, hi, _ = STREAMS[stream]
        if stream < 2:
            return w_aq.at[span(slot, 128), lo:hi]
        return w_aq.at[span(slot + 4, 128), 0 : hi - lo]

    scatters = [Scatter(place, (block_a, block_t)[s], bufs[s], sc_send.at[s], sc_recv.at[s]) for s in range(2)]
    unit_a, unit_t = units.at[0], units.at[1]
    gm_a, gm_t = gms.at[0], gms.at[1]
    mixed_a, mixed_t = mixeds.at[0], mixeds.at[1]
    seqs = [slice(0, 128), slice(128, 256)]

    with jax.named_scope("tokens_to_agents"):
        tokens_in.start()
        loads[0].wait()
        swap_rows(cot, turned)
        cot_in.start()
        self_t = lax.broadcasted_iota(jnp.int32, (128, 128), 0) == lax.broadcasted_iota(jnp.int32, (128, 128), 1)
        for a in range(2):
            row = observed[pl.ds(place.ag * 16 + place.tm * 2 + a, 1), :]
            bias_t[a] = jnp.where((row > 0) | self_t, 0.0, masked_score)
        at_step = lax.broadcasted_iota(jnp.int32, (8, STEPS), 1) == place.tm * 16 + place.ag
        seen = matmul(jnp.where(at_step, 1.0, 0.0).astype(BF), observed[...].astype(F32).astype(BF), NT)
        self_a = lax.broadcasted_iota(jnp.int32, (256, 256), 0) == lax.broadcasted_iota(jnp.int32, (256, 256), 1)
        bias_a[...] = jnp.where((seen[0:1, :] > 0.5) | self_a, 0.0, masked_score)
        loads[1].wait()
        tokens_in.wait()
    with jax.named_scope("time_forward"):
        project(x_time, unit_t, w_tq, merged_t)
        twins[1].copy(0, unit_t).start()
        for a in range(2):
            attend(merged_t, mixed_t, seqs[a], bias_t.at[a])
        twins[1].copy(2, mixed_t).start()
        loads[2].wait()
        add_residual(x_time, mixed_t, w_to, made, (2, 128))
        first_home.start()
    with jax.named_scope("first_to_steps"):
        cot_in.wait()
        twins[0].copy(3, g_agent).start()
        loads[3].wait()
        grad_of_mixed(g_agent.at[0:256, :], w_ao, gmix)
        cot_in.drain()
        first_home.wait()
        swap_rows(home, turned)
        first_agent.start()
        loads[4].wait()
        first_agent.wait()
    with jax.named_scope("agent_backward"):
        project(x_agent, unit_a, w_aq, merged_a)
        twins[0].copy(0, unit_a).start()
        attend_back(merged_a, gmix, mixed_a, gm_a, slice(0, 256), bias_a)
        twins[0].copy(2, mixed_a).start()
        twins[0].copy(1, gm_a).start()
        grad_of_input(x_agent, g_agent.at[0:256, :], gm_a, w_aq, gu, cot, (256,))
        back_home.start()
    with jax.named_scope("agent_weights"):
        for slot, ref in enumerate((unit_a, gm_a, mixed_a, g_agent)):
            twins[0].copy(slot, ref).wait_recv()
        transposed(place, unit_a, mixed_a, ut, ut_mixed)
        for stream in range(3):
            scatters[0].start(stream, ut, ut_mixed, gm_a, g_agent)
    with jax.named_scope("grad_first_to_agents"):
        back_home.wait()
        swap_rows(back, home)
        back_time.start()
        back_time.wait()
        twins[1].copy_rows(3, g_time).start()
    with jax.named_scope("time_backward"):
        g_own = g_time.at[0:2]
        grad_of_mixed(g_own, w_to, gmix)
        for a in range(2):
            attend_back(merged_t, gmix, None, gm_t, seqs[a], bias_t.at[a])
        twins[1].copy(1, gm_t).start()
        first_home.drain()
        grad_of_input(x_time, g_own, gm_t, w_tq, gu, made, (2, 128))
        tokens_out.start()
    with jax.named_scope("time_weights"):
        for slot, ref in enumerate((unit_t, gm_t, mixed_t)):
            twins[1].copy(slot, ref).wait_recv()
        twins[1].copy_rows(3, g_time).wait_recv()
        transposed(place, unit_t, mixed_t, ut, ut_mixed)
        for stream in range(3):
            scatters[1].start(stream, ut, ut_mixed, gm_t, g_time)
    with jax.named_scope("rings"):
        outs = ((aq_ref, ao_ref), (tq_ref, to_ref))
        for stream in range(3):
            scatters[0].second(stream)
        for stream in range(3):
            scatters[0].third(stream)
        for stream in range(3):
            scatters[1].second(stream)
        for stream in range(3):
            scatters[0].last(stream, *outs[0])
        for stream in range(3):
            scatters[1].third(stream)
        for stream in range(3):
            scatters[1].last(stream, *outs[1])
        tokens_out.wait()
    with jax.named_scope("drain"):
        for s in range(2):
            scatters[s].drain()
        for slot, ref in enumerate((unit_a, gm_a, mixed_a, g_agent)):
            twins[0].copy(slot, ref).wait_send()
        for slot, ref in enumerate((unit_t, gm_t, mixed_t)):
            twins[1].copy(slot, ref).wait_send()
        twins[1].copy_rows(3, g_time).wait_send()
        for moved in (tokens_in, first_agent, back_home, back_time, tokens_out):
            moved.drain()


def local(tokens, cotangent, observed, time_qkv, time_out, agent_qkv, agent_out):
    shape = jax.ShapeDtypeStruct
    grad_tokens, *grads = pl.pallas_call(
        block_kernel,
        out_shape=[
            shape((16, 16, D), BF),
            shape((8, 3 * D), F32),
            shape((8, D), F32),
            shape((8, 3 * D), F32),
            shape((8, D), F32),
        ],
        in_specs=[
            pl.BlockSpec(memory_space=pl.ANY),
            pl.BlockSpec(memory_space=pl.ANY),
            pl.BlockSpec(memory_space=pltpu.VMEM),
        ]
        + [pl.BlockSpec(memory_space=pl.ANY)] * 4,
        out_specs=[pl.BlockSpec(memory_space=pl.ANY)] + [pl.BlockSpec(memory_space=pltpu.VMEM)] * 4,
        scratch_shapes=[
            pltpu.VMEM((D, 3 * D), BF),
            pltpu.VMEM((D, D), BF),
            pltpu.VMEM((D, 3 * D), BF),
            pltpu.VMEM((D, D), BF),
            pltpu.VMEM((2, 128, D), BF),
            pltpu.VMEM((2, 128, D), BF),
            pltpu.VMEM((16, 16, D), BF),
            pltpu.VMEM((256, D), BF),
            pltpu.VMEM((256, D), BF),
            pltpu.VMEM((256, D), BF),
            pltpu.VMEM((256, D), BF),
            pltpu.VMEM((256, 3 * D), BF),
            pltpu.VMEM((256, 3 * D), BF),
            pltpu.VMEM((256, D), BF),
            pltpu.VMEM((256, D), F32),
            pltpu.VMEM((2, 128, 128), F32),
            pltpu.VMEM((256, 256), F32),
            pltpu.VMEM((2, 512, D), BF),
            pltpu.VMEM((2, 512, 3 * D), BF),
            pltpu.VMEM((2, 512, D), BF),
            pltpu.VMEM((4, 128, D), BF),
            pltpu.VMEM((512, D), BF),
            pltpu.VMEM((3, 512, 512), BF),
            pltpu.VMEM((512, 512), BF),
        ]
        + [pltpu.VMEM((3, 128, 4096), BF)]
        + scatter_bufs()
        + scatter_bufs()
        + [
            pltpu.SemaphoreType.DMA((5,)),
            pltpu.SemaphoreType.DMA((7, 16)),
            pltpu.SemaphoreType.DMA((7, 16)),
            pltpu.SemaphoreType.DMA((2, 4)),
            pltpu.SemaphoreType.DMA((2, 4)),
            pltpu.SemaphoreType.DMA((2, 3, 3, 3)),
            pltpu.SemaphoreType.DMA((2, 3, 3, 3)),
        ],
        compiler_params=pltpu.CompilerParams(
            collective_id=0, has_side_effects=True, vmem_limit_bytes=61 * 1024 * 1024
        ),
    )(
        tokens.reshape(16, 16, D),
        cotangent.reshape(256, D),
        observed.reshape(256, STEPS),
        time_qkv,
        time_out,
        agent_qkv,
        agent_out,
    )
    return (grad_tokens.reshape(1, 16, 16, D), *grads)


def solution(mesh):
    in_specs = (P(None, "ag", "tm", None), P(None, "ag", "tm", None), P(), P(), P(), P(), P())
    out_specs = (
        P(None, "ag", "tm", None),
        P(("ag", "tm"), None),
        P(("ag", "tm"), None),
        P(("ag", "tm"), None),
        P(("ag", "tm"), None),
    )
    return jax.shard_map(local, mesh=mesh, in_specs=in_specs, out_specs=out_specs, check_vma=False)
```

profile of v0, /device:TPU:0, one launch (start us, length us, event | category | flops | bytes accessed | tf_op | source)
XLA Modules:
  0.0 162.2 jit_solution(15732112430937612288)
XLA Ops:
  0.6 153.9 %shard_map.110 = (bf16[16,16,1024]{2,1,0:T(8,128)(2,1)}, f32[8,3072]{1,0:T(8,128)}, f32[8,1024]{1,0:T(8,128)}, f32[8,3072]{1,0:T(8,128)}, f32[8,1024]{1,0:T(8,128)}) custom-call(bf16[16,16,1024]{2,1,0:T(8,128)(2,1)} %bitcast.4, bf16[256,1024]{1,0:T(8,128)(2,1)} %bitcast.5, s32[256,128]{1,0:T(8,128)} %bitcast.7, bf16[1024,3072]{1,0:T(8,128)(2,1)} %time_qkv.1, ...), custom_call_target="tpu_custom_call" | custom-call | tf_op jit(solution)/shard_map/pallas_call | solution.py:553
  154.5 1.9 %copy.17 = bf16[1,16,16,1024]{3,2,1,0:T(8,128)(2,1)} copy(bf16[1,16,16,1024]{3,2,1,0:T(8,128)(2,1)} %bitcast.6) | data formatting | bytes 1048576
  156.4 1.5 copy.18
  158.0 1.4 copy.19
  159.3 1.5 copy.20
  160.9 1.4 copy.21
where the time goes:
time: 163 us; the launch traced here: 162 us
  Pallas kernels  154 us (94%)
  local copies, waits for them, and re-layouts  7.71 us (5%)
    pallas_call x1, Pallas kernels, local(): pl.pallas_call(block_kernel, out_shape=[shape((16, 16, D), BF), shape((8,...  154 us
    unnamed x5, local copies, waits for them, and re-layouts  7.71 us

commit v1 on v0

--- a/solution.py
+++ b/solution.py
@@ -20,7 +20,7 @@
 NT = (((1,), (1,)), ((), ()))
 TN = (((0,), (0,)), ((), ()))
 
-STREAMS = ((0, 1408, "xyz"), (1408, 2816, "yzx"), (2816, 4096, "zyx"))
+STREAMS = ((0, 1408, "xyz"), (1408, 2816, "yzx"), (2816, 4096, "zxy"))
 
 
 def matmul(left, right, dims=(((1,), (0,)), ((), ()))):
@@ -90,9 +90,9 @@
 
 
 class Scatter:
-    def __init__(self, place, block, bufs, send, recv):
-        self.place = place
-        self.block, (self.own, self.r1, self.s2, self.r2, self.s3, self.r3) = block, bufs
+    def __init__(self, place, block, second_block, bufs, send, recv):
+        self.place, self.second_block = place, second_block
+        self.block, (self.own, self.r1, self.r2, self.s3, self.r3) = block, bufs
         self.send, self.recv = send, recv
 
     def copy(self, stream, phase, step):
@@ -104,10 +104,10 @@
         if phase == 0:
             src, dst = self.block(stream, slot), self.r1.at[slot, :, cols]
         elif phase == 1:
-            src = self.s2.at[pl.ds(pl.multiple_of(to * 32, 32), 32), cols]
+            src = self.second_block(stream).at[pl.ds(pl.multiple_of(to * 32, 32), 32), :]
             dst = self.r2.at[slot, :, cols]
         else:
-            src = self.s3.at[pl.ds(pl.multiple_of(to * 8, 8), 8), cols]
+            src = self.s3.at[to, :, cols]
             dst = self.r3.at[slot, :, cols]
         return remote(
             src,
@@ -121,9 +121,9 @@
         lo, hi, _ = STREAMS[stream]
         rows = pl.ds(pl.multiple_of(block * 128, 128), 128)
         if stream < 2:
-            return [(lo, hi, matmul(ut[stream, rows, :], gm[:, lo:hi]))]
+            return [(lo, hi, matmul(ut[stream][rows, :], gm[:, lo:hi]))]
         return [
-            (lo, 3072, matmul(ut[2, rows, :], gm[:, lo:3072])),
+            (lo, 3072, matmul(ut[2][rows, :], gm[:, lo:3072])),
             (3072, 4096, matmul(ut_mixed[rows, :], g[...].reshape(512, D))),
         ]
 
@@ -152,7 +152,7 @@
             for slot in range(3):
                 total = total + self.r1[slot, rows, lo:hi].astype(F32)
             self.own[rows, lo:hi] = total
-            self.s2[rows, lo:hi] = total.astype(BF)
+            self.second_block(stream)[rows, :] = total.astype(BF)
             return carry
 
         lax.fori_loop(0, 4, one, 0)
@@ -166,7 +166,9 @@
         total = self.own[pl.ds(pl.multiple_of(self.place.at(axes[1]) * 32, 32), 32), lo:hi]
         for slot in range(3):
             total = total + self.r2[slot, :, lo:hi].astype(F32)
-        self.s3[:, lo:hi] = total
+        self.own[0:32, lo:hi] = total
+        for q in range(4):
+            self.s3[q, :, lo:hi] = total[q * 8 : q * 8 + 8].astype(BF)
         for step in (1, 2, 3):
             self.copy(stream, 2, step).start()
 
@@ -174,9 +176,9 @@
         lo, hi, axes = STREAMS[stream]
         for step in (1, 2, 3):
             self.copy(stream, 2, step).wait_recv()
-        total = self.s3[pl.ds(pl.multiple_of(self.place.at(axes[2]) * 8, 8), 8), lo:hi]
+        total = self.own[pl.ds(pl.multiple_of(self.place.at(axes[2]) * 8, 8), 8), lo:hi]
         for slot in range(3):
-            total = total + self.r3[slot, :, lo:hi]
+            total = total + self.r3[slot, :, lo:hi].astype(F32)
         top = min(hi, 3072)
         qkv_ref[:, lo:top] = total[:, : top - lo]
         if hi > 3072:
@@ -193,28 +195,36 @@
     return [
         pltpu.VMEM((128, 4096), F32),
         pltpu.VMEM((3, 128, 4096), BF),
-        pltpu.VMEM((128, 4096), BF),
         pltpu.VMEM((3, 32, 4096), BF),
-        pltpu.VMEM((32, 4096), F32),
-        pltpu.VMEM((3, 8, 4096), F32),
+        pltpu.VMEM((4, 8, 4096), BF),
+        pltpu.VMEM((3, 8, 4096), BF),
     ]
 
 
-def transposed(place, unit, mixed, ut, ut_mixed):
+def transposed(place, unit, mixed, ut, ut_mixed, spare):
     sel_x = selector(place.core, True)
     sel_z = selector(place.core, False)
+
+    def last_order(part, y):
+        for z in range(4):
+            for x in range(4):
+                at = (z % 2) * 128 + x * 32 + y * 8
+                spare[at : at + 8, (z // 2) * 512 : (z // 2) * 512 + 512] = part[z * 32 + x * 8 : z * 32 + x * 8 + 8]
+
     for y in range(4):
         cols = slice(y * 256, y * 256 + 256)
         part = matmul(sel_x, unit[:, cols], NT).astype(BF)
         for x in range(4):
-            ut[0, x * 128 + y * 32 : x * 128 + y * 32 + 32, :] = part[x * 32 : x * 32 + 32]
-        part = matmul(sel_z, unit[:, cols], NT).astype(BF)
-        ut[1, y * 128 : y * 128 + 128, :] = part
-        for z in range(4):
-            ut[2, z * 128 + y * 32 : z * 128 + y * 32 + 32, :] = part[z * 32 : z * 32 + 32]
-        part = matmul(sel_z, mixed[:, cols], NT).astype(BF)
-        for z in range(4):
-            ut_mixed[z * 128 + y * 32 : z * 128 + y * 32 + 32, :] = part[z * 32 : z * 32 + 32]
+            ut[0][x * 128 + y * 32 : x * 128 + y * 32 + 32, :] = part[x * 32 : x * 32 + 32]
+        part = matmul(sel_z, unit[:, cols], NT)
+        ut[1][y * 128 : y * 128 + 128, :] = part.astype(BF)
+        last_order(part, y)
+    ut[2][0:256, :] = spare[:, 0:512].astype(BF)
+    ut[2][256:512, :] = spare[:, 512:1024].astype(BF)
+    for y in range(4):
+        last_order(matmul(sel_z, mixed[:, y * 256 : y * 256 + 256], NT), y)
+    ut_mixed[0:256, :] = spare[:, 0:512].astype(BF)
+    ut_mixed[256:512, :] = spare[:, 512:1024].astype(BF)
 
 
 def normal(x_ref):
@@ -251,51 +261,66 @@
     return q, k, v
 
 
-def prob_of(q, k, bias):
-    scores = matmul(q, k, NT) + bias
-    shifted = jnp.exp(scores - jnp.max(scores, axis=-1, keepdims=True))
-    return shifted * (1.0 / jnp.sum(shifted, axis=-1, keepdims=True))
-
-
-def attend(merged, mixed, rows, bias_ref):
-    def one(pair, carry):
-        q, k, v = pair_parts(merged, rows, pair)
-        total = None
-        for half in halves():
-            part = matmul(prob_of(q * half, k, bias_ref[...]).astype(BF), v * half)
-            total = part if total is None else total + part
-        mixed[rows, span(pair, 128)] = total.astype(BF)
+def attend(merged, mixed, seqs, biases, group):
+    def one(turn, carry):
+        low_high = halves()
+        jobs = []
+        for rows, bias in zip(seqs, biases):
+            for i in range(group):
+                pair = turn * group + i
+                q, k, v = pair_parts(merged, rows, pair)
+                for half in low_high:
+                    jobs.append((rows, pair, bias, q * half, k, v * half))
+        scores = [matmul(q, k, NT) + bias[...] for _, _, bias, q, k, _ in jobs]
+        probs = probs_of(scores)
+        parts = [matmul(p.astype(BF), job[5]) for p, job in zip(probs, jobs)]
+        for i in range(0, len(jobs), 2):
+            rows, pair = jobs[i][:2]
+            mixed[rows, span(pair, 128)] = (parts[i] + parts[i + 1]).astype(BF)
         return carry
 
-    lax.fori_loop(0, H // 2, one, 0)
-
-
-def attend_back(merged, gmix, mixed, gm, rows, bias_ref):
-    def one(pair, carry):
-        q, k, v = pair_parts(merged, rows, pair)
-        go = gmix[rows, span(pair, 128)]
-        sums = [None] * 4
-        for half in halves():
-            prob = prob_of(q * half, k, bias_ref[...])
-            rounded = prob.astype(BF)
-            go_half = go * half
-            gp = matmul(go_half, v, NT)
-            gs = (prob * (gp - jnp.sum(gp * prob, axis=-1, keepdims=True))).astype(BF)
-            parts = [
-                matmul(gs, k * half),
-                matmul(gs, q * half, TN),
-                matmul(rounded, go_half, TN),
-                None if mixed is None else matmul(rounded, v * half),
-            ]
-            sums = [p if s is None else s + p for s, p in zip(sums, parts)]
-        gm[rows, span(pair, 128)] = (sums[0] * HD**-0.5).astype(BF)
-        gm[rows, pl.ds(pl.multiple_of(D + pair * 128, 128), 128)] = sums[1].astype(BF)
-        gm[rows, pl.ds(pl.multiple_of(2 * D + pair * 128, 128), 128)] = sums[2].astype(BF)
+    lax.fori_loop(0, H // 2 // group, one, 0)
+
+
+def probs_of(scores):
+    tops = [jnp.max(s, axis=-1, keepdims=True) for s in scores]
+    shifted = [jnp.exp(s - t) for s, t in zip(scores, tops)]
+    sums = [jnp.sum(s, axis=-1, keepdims=True) for s in shifted]
+    return [s * (1.0 / t) for s, t in zip(shifted, sums)]
+
+
+def attend_back(merged, gmix, mixed, gm, seqs, biases, group):
+    def one(turn, carry):
+        low_high = halves()
+        jobs = []
+        for rows, bias in zip(seqs, biases):
+            for i in range(group):
+                pair = turn * group + i
+                q, k, v = pair_parts(merged, rows, pair)
+                go = gmix[rows, span(pair, 128)]
+                for half in low_high:
+                    jobs.append((rows, pair, bias, q * half, k, v, go * half, half))
+        scores = [matmul(job[3], job[4], NT) + job[2][...] for job in jobs]
+        gps = [matmul(job[6], job[5], NT) for job in jobs]
+        probs = probs_of(scores)
+        means = [jnp.sum(gp * p, axis=-1, keepdims=True) for gp, p in zip(gps, probs)]
+        gss = [(p * (gp - m)).astype(BF) for p, gp, m in zip(probs, gps, means)]
+        rounded = [p.astype(BF) for p in probs]
+        gq = [matmul(gs, job[4] * job[7]) for gs, job in zip(gss, jobs)]
+        gk = [matmul(gs, job[3], TN) for gs, job in zip(gss, jobs)]
+        gv = [matmul(p, job[6], TN) for p, job in zip(rounded, jobs)]
         if mixed is not None:
-            mixed[rows, span(pair, 128)] = sums[3].astype(BF)
+            mx = [matmul(p, job[5] * job[7]) for p, job in zip(rounded, jobs)]
+        for i in range(0, len(jobs), 2):
+            rows, pair = jobs[i][:2]
+            gm[rows, span(pair, 128)] = ((gq[i] + gq[i + 1]) * HD**-0.5).astype(BF)
+            gm[rows, pl.ds(pl.multiple_of(D + pair * 128, 128), 128)] = (gk[i] + gk[i + 1]).astype(BF)
+            gm[rows, pl.ds(pl.multiple_of(2 * D + pair * 128, 128), 128)] = (gv[i] + gv[i + 1]).astype(BF)
+            if mixed is not None:
+                mixed[rows, span(pair, 128)] = (mx[i] + mx[i + 1]).astype(BF)
         return carry
 
-    lax.fori_loop(0, H // 2, one, 0)
+    lax.fori_loop(0, H // 2 // group, one, 0)
 
 
 def add_residual(x_ref, mixed, w, out_ref, shape):
@@ -383,12 +408,12 @@
     w_tq, w_to, w_aq, w_ao,
     x_time, made, home, turned, x_agent, cot, back,
     merged_t, merged_a, gmix, gu, bias_t, bias_a,
-    units, gms, mixeds, g_time, g_agent, ut, ut_mixed,
+    units, gms, mixeds, g_time, g_agent,
     *rest,
 ):
     grad_a = rest[0]
-    bufs = (rest[1:7], rest[7:13])
-    load, swap_send, swap_recv, twin_send, twin_recv, sc_send, sc_recv = rest[13:]
+    bufs = (rest[1:6], rest[6:11])
+    load, swap_send, swap_recv, twin_send, twin_recv, sc_send, sc_recv = rest[11:]
     place = Place()
     loads = [
         pltpu.make_async_copy(src, dst, load.at[i])
@@ -444,11 +469,25 @@
             return w_aq.at[span(slot, 128), lo:hi]
         return w_aq.at[span(slot + 4, 128), 0 : hi - lo]
 
-    scatters = [Scatter(place, (block_a, block_t)[s], bufs[s], sc_send.at[s], sc_recv.at[s]) for s in range(2)]
+    def second_a(stream):
+        lo, hi, _ = STREAMS[stream]
+        return w_aq.at[512 + stream * 128 : 640 + stream * 128, 1408 : 1408 + hi - lo]
+
+    def second_t(stream):
+        lo, hi, _ = STREAMS[stream]
+        if stream < 2:
+            return w_aq.at[384:512, lo:hi]
+        return w_aq.at[896:1024, 0 : hi - lo]
+
+    blocks, seconds = (block_a, block_t), (second_a, second_t)
+    scatters = [Scatter(place, blocks[s], seconds[s], bufs[s], sc_send.at[s], sc_recv.at[s]) for s in range(2)]
     unit_a, unit_t = units.at[0], units.at[1]
     gm_a, gm_t = gms.at[0], gms.at[1]
     mixed_a, mixed_t = mixeds.at[0], mixeds.at[1]
+    ut = [w_ao.at[0:512, 0:512], w_ao.at[0:512, 512:1024], w_ao.at[512:1024, 0:512]]
+    ut_mixed = w_ao.at[512:1024, 512:1024]
     seqs = [slice(0, 128), slice(128, 256)]
+    biases_t = [bias_t.at[0], bias_t.at[1]]
 
     with jax.named_scope("tokens_to_agents"):
         tokens_in.start()
@@ -468,8 +507,7 @@
     with jax.named_scope("time_forward"):
         project(x_time, unit_t, w_tq, merged_t)
         twins[1].copy(0, unit_t).start()
-        for a in range(2):
-            attend(merged_t, mixed_t, seqs[a], bias_t.at[a])
+        attend(merged_t, mixed_t, seqs, biases_t, 4)
         twins[1].copy(2, mixed_t).start()
         loads[2].wait()
         add_residual(x_time, mixed_t, w_to, made, (2, 128))
@@ -488,7 +526,7 @@
     with jax.named_scope("agent_backward"):
         project(x_agent, unit_a, w_aq, merged_a)
         twins[0].copy(0, unit_a).start()
-        attend_back(merged_a, gmix, mixed_a, gm_a, slice(0, 256), bias_a)
+        attend_back(merged_a, gmix, mixed_a, gm_a, [slice(0, 256)], [bias_a], 2)
         twins[0].copy(2, mixed_a).start()
         twins[0].copy(1, gm_a).start()
         grad_of_input(x_agent, g_agent.at[0:256, :], gm_a, w_aq, gu, cot, (256,))
@@ -496,7 +534,7 @@
     with jax.named_scope("agent_weights"):
         for slot, ref in enumerate((unit_a, gm_a, mixed_a, g_agent)):
             twins[0].copy(slot, ref).wait_recv()
-        transposed(place, unit_a, mixed_a, ut, ut_mixed)
+        transposed(place, unit_a, mixed_a, ut, ut_mixed, gu)
         for stream in range(3):
             scatters[0].start(stream, ut, ut_mixed, gm_a, g_agent)
     with jax.named_scope("grad_first_to_agents"):
@@ -508,8 +546,7 @@
     with jax.named_scope("time_backward"):
         g_own = g_time.at[0:2]
         grad_of_mixed(g_own, w_to, gmix)
-        for a in range(2):
-            attend_back(merged_t, gmix, None, gm_t, seqs[a], bias_t.at[a])
+        attend_back(merged_t, gmix, None, gm_t, seqs, biases_t, 4)
         twins[1].copy(1, gm_t).start()
         first_home.drain()
         grad_of_input(x_time, g_own, gm_t, w_tq, gu, made, (2, 128))
@@ -518,7 +555,7 @@
         for slot, ref in enumerate((unit_t, gm_t, mixed_t)):
             twins[1].copy(slot, ref).wait_recv()
         twins[1].copy_rows(3, g_time).wait_recv()
-        transposed(place, unit_t, mixed_t, ut, ut_mixed)
+        transposed(place, unit_t, mixed_t, ut, ut_mixed, gu)
         for stream in range(3):
             scatters[1].start(stream, ut, ut_mixed, gm_t, g_time)
     with jax.named_scope("rings"):
@@ -546,6 +583,14 @@
         twins[1].copy_rows(3, g_time).wait_send()
         for moved in (tokens_in, first_agent, back_home, back_time, tokens_out):
             moved.drain()
+
+
+def hand_on(*refs):
+    copies = [pltpu.make_async_copy(refs[i], refs[5 + i], refs[10].at[i]) for i in range(5)]
+    for copy in copies:
+        copy.start()
+    for copy in copies:
+        copy.wait()
 
 
 def local(tokens, cotangent, observed, time_qkv, time_out, agent_qkv, agent_out):
@@ -589,8 +634,6 @@
             pltpu.VMEM((2, 512, D), BF),
             pltpu.VMEM((4, 128, D), BF),
             pltpu.VMEM((512, D), BF),
-            pltpu.VMEM((3, 512, 512), BF),
-            pltpu.VMEM((512, 512), BF),
         ]
         + [pltpu.VMEM((3, 128, 4096), BF)]
         + scatter_bufs()
@@ -616,6 +659,14 @@
         agent_qkv,
         agent_out,
     )
+    made = [grad_tokens, *grads]
+    grad_tokens, *grads = pl.pallas_call(
+        hand_on,
+        out_shape=[shape(x.shape, x.dtype) for x in made],
+        in_specs=[pl.BlockSpec(memory_space=pl.ANY)] * 5,
+        out_specs=[pl.BlockSpec(memory_space=pl.ANY)] * 5,
+        scratch_shapes=[pltpu.SemaphoreType.DMA((5,))],
+    )(*made)
     return (grad_tokens.reshape(1, 16, 16, D), *grads)
 
 

time: 163 us -> 162 us (level)
  local copies, waits for them, and re-layouts: 7.71 us -> 0 us
  Pallas kernels: 154 us -> 161 us
    pallas_call x0 -> x1, Pallas kernels: none -> 25 us  [local(): pl.pallas_call(hand_on, out_shape=[shape(x.shape, x.dtype) for x in made]...]
    pallas_call x1, Pallas kernels: 154 us -> 136 us  [local(): pl.pallas_call(block_kernel, out_shape=[shape((16, 16, D), BF), shape((8,...]
    unnamed x5 -> x0, local copies, waits for them, and re-layouts: 7.71 us -> none
where the time goes in v1:
time: 162 us; the launch traced here: 161 us
  Pallas kernels  161 us (99%)
    pallas_call x1, Pallas kernels, local(): pl.pallas_call(block_kernel, out_shape=[shape((16, 16, D), BF), shape((8,...  136 us
    pallas_call x1, Pallas kernels, local(): pl.pallas_call(hand_on, out_shape=[shape(x.shape, x.dtype) for x in made]...  25 us

profile of v1, /device:TPU:0, one launch (start us, length us, event | category | flops | bytes accessed | tf_op | source)
XLA Modules:
  0.0 161.4 jit_solution(15984731371670805079)
XLA Ops:
  0.6 135.6 %shard_map.110 = (bf16[16,16,1024]{2,1,0:T(8,128)(2,1)}, f32[8,3072]{1,0:T(8,128)}, f32[8,1024]{1,0:T(8,128)}, f32[8,3072]{1,0:T(8,128)}, f32[8,1024]{1,0:T(8,128)}) custom-call(bf16[16,16,1024]{2,1,0:T(8,128)(2,1)} %bitcast.4, bf16[256,1024]{1,0:T(8,128)(2,1)} %bitcast.5, s32[256,128]{1,0:T(8,128)} %bitcast.6, bf16[1024,3072]{1,0:T(8,128)(2,1)} %time_qkv.1, ...), custom_call_target="tpu_custom_call" | custom-call | tf_op jit(solution)/shard_map/pallas_call | solution.py:598
  136.3 25.0 %shard_map.111 = (bf16[16,16,1024]{2,1,0:T(8,128)(2,1)}, f32[8,3072]{1,0:T(8,128)}, f32[8,1024]{1,0:T(8,128)}, f32[8,3072]{1,0:T(8,128)}, f32[8,1024]{1,0:T(8,128)}) custom-call(bf16[16,16,1024]{2,1,0:T(8,128)(2,1)} %get-tuple-element.15.refs_0_, f32[8,3072]{1,0:T(8,128)} %get-tuple-element.16.refs_1_, f32[8,1024]{1,0:T(8,128)} %get-tuple-element.17.refs_2_, ...), custom_call_target="tpu_custom_call" | custom-call | tf_op jit(solution)/shard_map/pallas_call | solution.py:663

commit v2 on v1

--- a/solution.py
+++ b/solution.py
@@ -402,18 +402,118 @@
         lax.fori_loop(1, self.size, one, 0)
 
 
+def spread_index():
+    at = lax.broadcasted_iota(jnp.int32, (256, 256), 0)
+    row = lax.broadcasted_iota(jnp.int32, (256, 256), 1)
+    return at, row
+
+
+def one_hot(wanted, row):
+    return jnp.where(row == wanted, 1.0, 0.0).astype(BF)
+
+
+def pack_time(src, dst):
+    at, row = spread_index()
+    i, c, a = at // 16, (at // 2) % 8, at % 2
+    turn = one_hot(c * 32 + a * 16 + i, row)
+
+    def one(n, carry):
+        rows = span(n, 16)
+        parts = [src[a, rows, c * 128 : c * 128 + 128] for c in range(8) for a in range(2)]
+        out = matmul(turn, jnp.concatenate(parts, axis=0)).astype(BF)
+        dst[rows] = out.reshape(16, 16, 128)
+        return carry
+
+    lax.fori_loop(0, 8, one, 0)
+
+
+def unpack_time(src, dst):
+    at, row = spread_index()
+    c, a, i = at // 32, (at // 16) % 2, at % 16
+    turn = one_hot(i * 16 + c * 2 + a, row)
+
+    def one(n, carry):
+        rows = span(n, 16)
+        out = matmul(turn, src[rows].reshape(256, 128)).astype(BF)
+        for c in range(8):
+            for a in range(2):
+                part = out[c * 32 + a * 16 : c * 32 + a * 16 + 16]
+                dst[a, rows, c * 128 : c * 128 + 128] = part
+        return carry
+
+    lax.fori_loop(0, 8, one, 0)
+
+
+def pack_agent(src, dst):
+    at, row = spread_index()
+    i, c, a = at // 16, (at // 2) % 8, at % 2
+    turn = one_hot(c * 32 + i * 2 + a, row)
+
+    def one(n, carry):
+        parts = [src[span(n, 32), c * 128 : c * 128 + 128] for c in range(8)]
+        out = matmul(turn, jnp.concatenate(parts, axis=0)).astype(BF)
+        dst[span(n, 16)] = out.reshape(16, 16, 128)
+        return carry
+
+    lax.fori_loop(0, 8, one, 0)
+
+
+def unpack_agent(src, dst):
+    at, row = spread_index()
+    c, i, a = at // 32, (at // 2) % 16, at % 2
+    turn = one_hot(i * 16 + c * 2 + a, row)
+
+    def one(n, carry):
+        out = matmul(turn, src[span(n, 16)].reshape(256, 128)).astype(BF)
+        for c in range(8):
+            dst[span(n, 32), c * 128 : c * 128 + 128] = out[c * 32 : c * 32 + 32]
+        return carry
+
+    lax.fori_loop(0, 8, one, 0)
+
+
+class Spread:
+    def __init__(self, place, send, recv, src, dst, to_steps):
+        self.place, self.send, self.recv, self.src, self.dst, self.to_steps = place, send, recv, src, dst, to_steps
+
+    def places(self, ag, tm):
+        return ag * 8 + tm, tm * 16 + ag
+
+    def start(self):
+        place = self.place
+        agents, steps = self.places(place.ag, place.tm)
+        mine = agents if self.to_steps else steps
+
+        def one(step, carry):
+            ag, tm = (place.ag + step // 8) % 16, (place.tm + step % 8) % 8
+            by_agents, by_steps = self.places(ag, tm)
+            theirs = by_steps if self.to_steps else by_agents
+            remote(self.src.at[theirs], self.dst.at[mine], self.send, self.recv, (ag, tm)).start()
+            return carry
+
+        lax.fori_loop(1, 128, one, 0)
+        own = steps if self.to_steps else agents
+        pltpu.make_async_copy(self.src.at[own], self.dst.at[mine], self.recv).start()
+
+    def wait(self):
+        pltpu.make_async_copy(self.src, self.dst, self.recv).wait()
+
+    def drain(self):
+        pltpu.make_async_copy(self.src.at[0:127], self.dst.at[0:127], self.send).wait()
+
+
 def block_kernel(
     tokens, cotangent, observed, time_qkv, time_out, agent_qkv, agent_out,
     grad_tokens, tq_ref, to_ref, aq_ref, ao_ref,
     w_tq, w_to, w_aq, w_ao,
-    x_time, made, home, turned, x_agent, cot, back,
+    x_time, made, turned, x_agent, cot, tiles_out, first_in, back_in,
     merged_t, merged_a, gmix, gu, bias_t, bias_a,
     units, gms, mixeds, g_time, g_agent,
     *rest,
 ):
     grad_a = rest[0]
     bufs = (rest[1:6], rest[6:11])
-    load, swap_send, swap_recv, twin_send, twin_recv, sc_send, sc_recv = rest[11:]
+    load, spread_send, spread_recv, swap_send, swap_recv, twin_send, twin_recv, sc_send, sc_recv = rest[11:]
     place = Place()
     loads = [
         pltpu.make_async_copy(src, dst, load.at[i])
@@ -452,11 +552,9 @@
 
     tokens_in = swap(0, "tm", two(tokens), sixteen(x_time))
     cot_in = swap(1, "ag", rows16(turned), rows16(g_agent))
-    first_home = swap(2, "tm", sixteen(made), two(home))
-    first_agent = swap(3, "ag", rows16(turned), rows16(x_agent))
-    back_home = swap(4, "ag", rows16(cot), rows16(back))
-    back_time = swap(5, "tm", two(home), sixteen(g_time))
-    tokens_out = swap(6, "tm", sixteen(made), two(grad_tokens))
+    first = Spread(place, spread_send.at[0], spread_recv.at[0], tiles_out, first_in, True)
+    back = Spread(place, spread_send.at[1], spread_recv.at[1], tiles_out, back_in, False)
+    tokens_out = swap(2, "tm", sixteen(made), two(grad_tokens))
     twins = [Twin(place, twin_send.at[s], twin_recv.at[s]) for s in range(2)]
 
     def block_a(stream, slot):
@@ -511,18 +609,17 @@
         twins[1].copy(2, mixed_t).start()
         loads[2].wait()
         add_residual(x_time, mixed_t, w_to, made, (2, 128))
-        first_home.start()
+        pack_time(made, tiles_out)
+        first.start()
     with jax.named_scope("first_to_steps"):
         cot_in.wait()
         twins[0].copy(3, g_agent).start()
         loads[3].wait()
         grad_of_mixed(g_agent.at[0:256, :], w_ao, gmix)
         cot_in.drain()
-        first_home.wait()
-        swap_rows(home, turned)
-        first_agent.start()
         loads[4].wait()
-        first_agent.wait()
+        first.wait()
+        unpack_agent(first_in, x_agent)
     with jax.named_scope("agent_backward"):
         project(x_agent, unit_a, w_aq, merged_a)
         twins[0].copy(0, unit_a).start()
@@ -530,7 +627,9 @@
         twins[0].copy(2, mixed_a).start()
         twins[0].copy(1, gm_a).start()
         grad_of_input(x_agent, g_agent.at[0:256, :], gm_a, w_aq, gu, cot, (256,))
-        back_home.start()
+        first.drain()
+        pack_agent(cot, tiles_out)
+        back.start()
     with jax.named_scope("agent_weights"):
         for slot, ref in enumerate((unit_a, gm_a, mixed_a, g_agent)):
             twins[0].copy(slot, ref).wait_recv()
@@ -538,17 +637,14 @@
         for stream in range(3):
             scatters[0].start(stream, ut, ut_mixed, gm_a, g_agent)
     with jax.named_scope("grad_first_to_agents"):
-        back_home.wait()
-        swap_rows(back, home)
-        back_time.start()
-        back_time.wait()
+        back.wait()
+        unpack_time(back_in, g_time)
         twins[1].copy_rows(3, g_time).start()
     with jax.named_scope("time_backward"):
         g_own = g_time.at[0:2]
         grad_of_mixed(g_own, w_to, gmix)
         attend_back(merged_t, gmix, None, gm_t, seqs, biases_t, 4)
         twins[1].copy(1, gm_t).start()
-        first_home.drain()
         grad_of_input(x_time, g_own, gm_t, w_tq, gu, made, (2, 128))
         tokens_out.start()
     with jax.named_scope("time_weights"):
@@ -581,16 +677,13 @@
         for slot, ref in enumerate((unit_t, gm_t, mixed_t)):
             twins[1].copy(slot, ref).wait_send()
         twins[1].copy_rows(3, g_time).wait_send()
-        for moved in (tokens_in, first_agent, back_home, back_time, tokens_out):
+        for moved in (tokens_in, back, tokens_out):
             moved.drain()
 
 
 def hand_on(*refs):
-    copies = [pltpu.make_async_copy(refs[i], refs[5 + i], refs[10].at[i]) for i in range(5)]
-    for copy in copies:
-        copy.start()
-    for copy in copies:
-        copy.wait()
+    for source, target in zip(refs[:5], refs[5:]):
+        target[...] = source[...]
 
 
 def local(tokens, cotangent, observed, time_qkv, time_out, agent_qkv, agent_out):
@@ -618,11 +711,12 @@
             pltpu.VMEM((D, D), BF),
             pltpu.VMEM((2, 128, D), BF),
             pltpu.VMEM((2, 128, D), BF),
-            pltpu.VMEM((16, 16, D), BF),
             pltpu.VMEM((256, D), BF),
             pltpu.VMEM((256, D), BF),
             pltpu.VMEM((256, D), BF),
-            pltpu.VMEM((256, D), BF),
+            pltpu.VMEM((128, 16, 128), BF),
+            pltpu.VMEM((128, 16, 128), BF),
+            pltpu.VMEM((128, 16, 128), BF),
             pltpu.VMEM((256, 3 * D), BF),
             pltpu.VMEM((256, 3 * D), BF),
             pltpu.VMEM((256, D), BF),
@@ -640,8 +734,10 @@
         + scatter_bufs()
         + [
             pltpu.SemaphoreType.DMA((5,)),
-            pltpu.SemaphoreType.DMA((7, 16)),
-            pltpu.SemaphoreType.DMA((7, 16)),
+            pltpu.SemaphoreType.DMA((2,)),
+            pltpu.SemaphoreType.DMA((2,)),
+            pltpu.SemaphoreType.DMA((3, 16)),
+            pltpu.SemaphoreType.DMA((3, 16)),
             pltpu.SemaphoreType.DMA((2, 4)),
             pltpu.SemaphoreType.DMA((2, 4)),
             pltpu.SemaphoreType.DMA((2, 3, 3, 3)),
@@ -663,9 +759,8 @@
     grad_tokens, *grads = pl.pallas_call(
         hand_on,
         out_shape=[shape(x.shape, x.dtype) for x in made],
-        in_specs=[pl.BlockSpec(memory_space=pl.ANY)] * 5,
-        out_specs=[pl.BlockSpec(memory_space=pl.ANY)] * 5,
-        scratch_shapes=[pltpu.SemaphoreType.DMA((5,))],
+        in_specs=[pl.BlockSpec(memory_space=pltpu.VMEM)] * 5,
+        out_specs=[pl.BlockSpec(memory_space=pltpu.VMEM)] * 5,
     )(*made)
     return (grad_tokens.reshape(1, 16, 16, D), *grads)
 

time: 162 us -> 123 us (0.76)
  Pallas kernels: 161 us -> 122 us
    pallas_call x1, Pallas kernels: 25 us -> 2.02 us  [local(): pl.pallas_call(hand_on, out_shape=[shape(x.shape, x.dtype) for x in made]...]
    pallas_call x1, Pallas kernels: 136 us -> 120 us  [local(): pl.pallas_call(block_kernel, out_shape=[shape((16, 16, D), BF), shape((8,...]
where the time goes in v2:
time: 123 us
  Pallas kernels  122 us (99%)
    pallas_call x1, Pallas kernels, local(): pl.pallas_call(block_kernel, out_shape=[shape((16, 16, D), BF), shape((8,...  120 us

profile of v2, /device:TPU:0, one launch (start us, length us, event | category | flops | bytes accessed | tf_op | source)
XLA Modules:
  0.0 122.8 jit_solution(5405598710279224781)
XLA Ops:
  0.6 120.1 %shard_map.110 = (bf16[16,16,1024]{2,1,0:T(8,128)(2,1)}, f32[8,3072]{1,0:T(8,128)}, f32[8,1024]{1,0:T(8,128)}, f32[8,3072]{1,0:T(8,128)}, f32[8,1024]{1,0:T(8,128)}) custom-call(bf16[16,16,1024]{2,1,0:T(8,128)(2,1)} %bitcast.4, bf16[256,1024]{1,0:T(8,128)(2,1)} %bitcast.5, s32[256,128]{1,0:T(8,128)} %bitcast.6, bf16[1024,3072]{1,0:T(8,128)(2,1)} %time_qkv.1, ...), custom_call_target="tpu_custom_call" | custom-call | tf_op jit(solution)/shard_map/pallas_call | solution.py:691
  120.8 2.0 %shard_map.111 = (bf16[16,16,1024]{2,1,0:T(8,128)(2,1)}, f32[8,3072]{1,0:T(8,128)}, f32[8,1024]{1,0:T(8,128)}, f32[8,3072]{1,0:T(8,128)}, f32[8,1024]{1,0:T(8,128)}) custom-call(bf16[16,16,1024]{2,1,0:T(8,128)(2,1)} %get-tuple-element.15.refs_0_, f32[8,3072]{1,0:T(8,128)} %get-tuple-element.16.refs_1_, f32[8,1024]{1,0:T(8,128)} %get-tuple-element.17.refs_2_, ...), custom_call_target="tpu_custom_call" | custom-call | tf_op jit(solution)/shard_map/pallas_call | solution.py:759

commit v3 on v2

--- a/solution.py
+++ b/solution.py
@@ -92,8 +92,26 @@
 class Scatter:
     def __init__(self, place, block, second_block, bufs, send, recv):
         self.place, self.second_block = place, second_block
-        self.block, (self.own, self.r1, self.r2, self.s3, self.r3) = block, bufs
+        self.block, (self.own, self.r1, self.relay, self.r2, self.s3, self.r3) = block, bufs
         self.send, self.recv = send, recv
+
+    def first(self, stream, part):
+        lo, hi, axes = STREAMS[stream]
+        mid = (hi - lo) // 256 * 128
+        half_a, half_b = slice(0, mid), slice(mid, hi - lo)
+        all_a, all_b = slice(lo, lo + mid), slice(lo + mid, hi)
+        slot, near, far = (
+            (1, half_a, self.relay.at[:, all_a]),
+            (1, half_b, self.relay.at[:, all_b]),
+            (0, half_b, self.r1.at[0, :, all_b]),
+            (2, half_a, self.r1.at[1, :, all_a]),
+            (0, half_a, self.r1.at[0, :, all_a]),
+            (2, half_b, self.r1.at[1, :, all_b]),
+        )[part]
+        return remote(
+            self.block(stream, slot).at[:, near], far, self.send.at[stream, part], self.recv.at[stream, part],
+            self.place.ring(axes[0], 3 if part % 2 else 1),
+        )
 
     def copy(self, stream, phase, step):
         lo, hi, axes = STREAMS[stream]
@@ -101,20 +119,14 @@
         axis = axes[phase]
         to = (self.place.at(axis) + step) % 4
         slot = step - 1
-        if phase == 0:
-            src, dst = self.block(stream, slot), self.r1.at[slot, :, cols]
-        elif phase == 1:
+        if phase == 1:
             src = self.second_block(stream).at[pl.ds(pl.multiple_of(to * 32, 32), 32), :]
             dst = self.r2.at[slot, :, cols]
         else:
-            src = self.s3.at[to, :, cols]
-            dst = self.r3.at[slot, :, cols]
+            src, dst = self.s3.at[to, :, cols], self.r3.at[slot, :, cols]
+        sem = 3 + 3 * phase + slot
         return remote(
-            src,
-            dst,
-            self.send.at[stream, phase, slot],
-            self.recv.at[stream, phase, slot],
-            self.place.ring(axis, step),
+            src, dst, self.send.at[stream, sem], self.recv.at[stream, sem], self.place.ring(axis, step)
         )
 
     def product(self, stream, ut, ut_mixed, gm, g, block):
@@ -130,26 +142,33 @@
     def start(self, stream, ut, ut_mixed, gm, g):
         first, _, axes = STREAMS[stream]
         at = self.place.at(axes[0])
-
-        def one(step, carry):
-            for lo, hi, part in self.product(stream, ut, ut_mixed, gm, g, (at + step) % 4):
-                self.block(stream, step - 1)[:, lo - first : hi - first] = part.astype(BF)
-            self.copy(stream, 0, step).start()
-            return carry
-
-        lax.fori_loop(1, 4, one, 0)
-        for lo, hi, part in self.product(stream, ut, ut_mixed, gm, g, at):
-            self.own[:, lo:hi] = part
+        for step, parts in ((2, (0, 1)), (1, (2,)), (3, (3,))):
+            for lo, hi, made in self.product(stream, ut, ut_mixed, gm, g, (at + step) % 4):
+                self.block(stream, step - 1)[:, lo - first : hi - first] = made.astype(BF)
+            for part in parts:
+                self.first(stream, part).start()
+        for lo, hi, made in self.product(stream, ut, ut_mixed, gm, g, at):
+            self.own[:, lo:hi] = made
+
+    def pass_on(self, stream):
+        lo, hi, _ = STREAMS[stream]
+        mid = (hi - lo) // 256 * 128
+        for part, slot, left, right in ((0, 0, 0, mid), (1, 2, mid, hi - lo)):
+            self.first(stream, part).wait_recv()
+            block = self.block(stream, slot)
+            came = self.relay[:, lo + left : lo + right].astype(F32)
+            block[:, left:right] = (block[:, left:right].astype(F32) + came).astype(BF)
+            self.first(stream, part + 4).start()
 
     def second(self, stream):
         lo, hi, _ = STREAMS[stream]
-        for step in (1, 2, 3):
-            self.copy(stream, 0, step).wait_recv()
+        for part in (2, 3, 4, 5):
+            self.first(stream, part).wait_recv()
 
         def one(q, carry):
             rows = pl.ds(pl.multiple_of(q * 32, 32), 32)
             total = self.own[rows, lo:hi]
-            for slot in range(3):
+            for slot in range(2):
                 total = total + self.r1[slot, rows, lo:hi].astype(F32)
             self.own[rows, lo:hi] = total
             self.second_block(stream)[rows, :] = total.astype(BF)
@@ -186,7 +205,9 @@
 
     def drain(self):
         for stream in range(3):
-            for phase in range(3):
+            for part in range(6):
+                self.first(stream, part).wait_send()
+            for phase in (1, 2):
                 for step in (1, 2, 3):
                     self.copy(stream, phase, step).wait_send()
 
@@ -194,7 +215,8 @@
 def scatter_bufs():
     return [
         pltpu.VMEM((128, 4096), F32),
-        pltpu.VMEM((3, 128, 4096), BF),
+        pltpu.VMEM((2, 128, 4096), BF),
+        pltpu.VMEM((128, 4096), BF),
         pltpu.VMEM((3, 32, 4096), BF),
         pltpu.VMEM((4, 8, 4096), BF),
         pltpu.VMEM((3, 8, 4096), BF),
@@ -512,8 +534,8 @@
     *rest,
 ):
     grad_a = rest[0]
-    bufs = (rest[1:6], rest[6:11])
-    load, spread_send, spread_recv, swap_send, swap_recv, twin_send, twin_recv, sc_send, sc_recv = rest[11:]
+    bufs = (rest[1:7], rest[7:13])
+    load, spread_send, spread_recv, swap_send, swap_recv, twin_send, twin_recv, sc_send, sc_recv = rest[13:]
     place = Place()
     loads = [
         pltpu.make_async_copy(src, dst, load.at[i])
@@ -591,7 +613,6 @@
         tokens_in.start()
         loads[0].wait()
         swap_rows(cot, turned)
-        cot_in.start()
         self_t = lax.broadcasted_iota(jnp.int32, (128, 128), 0) == lax.broadcasted_iota(jnp.int32, (128, 128), 1)
         for a in range(2):
             row = observed[pl.ds(place.ag * 16 + place.tm * 2 + a, 1), :]
@@ -602,6 +623,7 @@
         bias_a[...] = jnp.where((seen[0:1, :] > 0.5) | self_a, 0.0, masked_score)
         loads[1].wait()
         tokens_in.wait()
+        cot_in.start()
     with jax.named_scope("time_forward"):
         project(x_time, unit_t, w_tq, merged_t)
         twins[1].copy(0, unit_t).start()
@@ -645,8 +667,12 @@
         grad_of_mixed(g_own, w_to, gmix)
         attend_back(merged_t, gmix, None, gm_t, seqs, biases_t, 4)
         twins[1].copy(1, gm_t).start()
+        for stream in range(3):
+            scatters[0].pass_on(stream)
         grad_of_input(x_time, g_own, gm_t, w_tq, gu, made, (2, 128))
         tokens_out.start()
+        for stream in range(3):
+            scatters[0].second(stream)
     with jax.named_scope("time_weights"):
         for slot, ref in enumerate((unit_t, gm_t, mixed_t)):
             twins[1].copy(slot, ref).wait_recv()
@@ -657,9 +683,9 @@
     with jax.named_scope("rings"):
         outs = ((aq_ref, ao_ref), (tq_ref, to_ref))
         for stream in range(3):
-            scatters[0].second(stream)
-        for stream in range(3):
             scatters[0].third(stream)
+        for stream in range(3):
+            scatters[1].pass_on(stream)
         for stream in range(3):
             scatters[1].second(stream)
         for stream in range(3):
@@ -740,8 +766,8 @@
             pltpu.SemaphoreType.DMA((3, 16)),
             pltpu.SemaphoreType.DMA((2, 4)),
             pltpu.SemaphoreType.DMA((2, 4)),
-            pltpu.SemaphoreType.DMA((2, 3, 3, 3)),
-            pltpu.SemaphoreType.DMA((2, 3, 3, 3)),
+            pltpu.SemaphoreType.DMA((2, 3, 12)),
+            pltpu.SemaphoreType.DMA((2, 3, 12)),
         ],
         compiler_params=pltpu.CompilerParams(
             collective_id=0, has_side_effects=True, vmem_limit_bytes=61 * 1024 * 1024

time: 123 us -> 111 us (0.902)
  Pallas kernels: 122 us -> 110 us
    pallas_call x1, Pallas kernels: 120 us -> 108 us  [local(): pl.pallas_call(block_kernel, out_shape=[shape((16, 16, D), BF), shape((8,...]
where the time goes in v3:
time: 111 us
  Pallas kernels  110 us (99%)
    pallas_call x1, Pallas kernels, local(): pl.pallas_call(block_kernel, out_shape=[shape((16, 16, D), BF), shape((8,...  108 us

profile of v3, /device:TPU:0, one launch (start us, length us, event | category | flops | bytes accessed | tf_op | source)
XLA Modules:
  0.0 110.8 jit_solution(10357034034109076327)
XLA Ops:
  0.6 108.1 %shard_map.110 = (bf16[16,16,1024]{2,1,0:T(8,128)(2,1)}, f32[8,3072]{1,0:T(8,128)}, f32[8,1024]{1,0:T(8,128)}, f32[8,3072]{1,0:T(8,128)}, f32[8,1024]{1,0:T(8,128)}) custom-call(bf16[16,16,1024]{2,1,0:T(8,128)(2,1)} %bitcast.4, bf16[256,1024]{1,0:T(8,128)(2,1)} %bitcast.5, s32[256,128]{1,0:T(8,128)} %bitcast.6, bf16[1024,3072]{1,0:T(8,128)(2,1)} %time_qkv.1, ...), custom_call_target="tpu_custom_call" | custom-call | tf_op jit(solution)/shard_map/pallas_call | solution.py:717
  108.7 2.0 %shard_map.111 = (bf16[16,16,1024]{2,1,0:T(8,128)(2,1)}, f32[8,3072]{1,0:T(8,128)}, f32[8,1024]{1,0:T(8,128)}, f32[8,3072]{1,0:T(8,128)}, f32[8,1024]{1,0:T(8,128)}) custom-call(bf16[16,16,1024]{2,1,0:T(8,128)(2,1)} %get-tuple-element.15.refs_0_, f32[8,3072]{1,0:T(8,128)} %get-tuple-element.16.refs_1_, f32[8,1024]{1,0:T(8,128)} %get-tuple-element.17.refs_2_, ...), custom_call_target="tpu_custom_call" | custom-call | tf_op jit(solution)/shard_map/pallas_call | solution.py:785

commit v4 on v3

--- a/solution.py
+++ b/solution.py
@@ -267,7 +267,7 @@
         merged[:, cols] = matmul(unit[0:256, :], w[:, cols]).astype(BF)
         return carry
 
-    lax.fori_loop(0, 6, one, 0)
+    lax.fori_loop(0, 6, one, 0, unroll=6)
 
 
 def halves():
@@ -359,16 +359,16 @@
         gmix[:, rows] = matmul(g[...].reshape(256, D), w[rows, :], NT).astype(BF)
         return carry
 
-    lax.fori_loop(0, 4, one, 0)
+    lax.fori_loop(0, 4, one, 0, unroll=4)
 
 
 def grad_of_input(x_ref, g, gm, w, gu, out_ref, shape):
     def one(n, carry):
-        rows = span(n, 256)
+        rows = span(n, 512)
         gu[:, rows] = matmul(gm[0:256, :], w[rows, :], NT)
         return carry
 
-    lax.fori_loop(0, 4, one, 0)
+    lax.fori_loop(0, 2, one, 0, unroll=2)
     normed, inverse = normal(x_ref)
     grad_unit = gu[...]
     rows = inverse * (grad_unit - normed * jnp.mean(grad_unit * normed, axis=-1, keepdims=True))
@@ -446,7 +446,7 @@
         dst[rows] = out.reshape(16, 16, 128)
         return carry
 
-    lax.fori_loop(0, 8, one, 0)
+    lax.fori_loop(0, 8, one, 0, unroll=8)
 
 
 def unpack_time(src, dst):
@@ -463,7 +463,7 @@
                 dst[a, rows, c * 128 : c * 128 + 128] = part
         return carry
 
-    lax.fori_loop(0, 8, one, 0)
+    lax.fori_loop(0, 8, one, 0, unroll=8)
 
 
 def pack_agent(src, dst):
@@ -477,7 +477,7 @@
         dst[span(n, 16)] = out.reshape(16, 16, 128)
         return carry
 
-    lax.fori_loop(0, 8, one, 0)
+    lax.fori_loop(0, 8, one, 0, unroll=8)
 
 
 def unpack_agent(src, dst):
@@ -491,7 +491,7 @@
             dst[span(n, 32), c * 128 : c * 128 + 128] = out[c * 32 : c * 32 + 32]
         return carry
 
-    lax.fori_loop(0, 8, one, 0)
+    lax.fori_loop(0, 8, one, 0, unroll=8)
 
 
 class Spread:
@@ -525,11 +525,11 @@
 
 
 def block_kernel(
-    tokens, cotangent, observed, time_qkv, time_out, agent_qkv, agent_out,
+    tokens, cotangent, observed_in, time_qkv, time_out, agent_qkv, agent_out,
     grad_tokens, tq_ref, to_ref, aq_ref, ao_ref,
     w_tq, w_to, w_aq, w_ao,
     x_time, made, turned, x_agent, cot, tiles_out, first_in, back_in,
-    merged_t, merged_a, gmix, gu, bias_t, bias_a,
+    merged_t, merged_a, gmix, gu, bias_t, bias_a, observed,
     units, gms, mixeds, g_time, g_agent,
     *rest,
 ):
@@ -542,6 +542,7 @@
         for i, (src, dst) in enumerate(
             (
                 (cotangent, cot),
+                (observed_in, observed),
                 (time_qkv, w_tq),
                 (time_out, w_to),
                 (agent_out, w_ao),
@@ -613,6 +614,7 @@
         tokens_in.start()
         loads[0].wait()
         swap_rows(cot, turned)
+        loads[1].wait()
         self_t = lax.broadcasted_iota(jnp.int32, (128, 128), 0) == lax.broadcasted_iota(jnp.int32, (128, 128), 1)
         for a in range(2):
             row = observed[pl.ds(place.ag * 16 + place.tm * 2 + a, 1), :]
@@ -621,7 +623,7 @@
         seen = matmul(jnp.where(at_step, 1.0, 0.0).astype(BF), observed[...].astype(F32).astype(BF), NT)
         self_a = lax.broadcasted_iota(jnp.int32, (256, 256), 0) == lax.broadcasted_iota(jnp.int32, (256, 256), 1)
         bias_a[...] = jnp.where((seen[0:1, :] > 0.5) | self_a, 0.0, masked_score)
-        loads[1].wait()
+        loads[2].wait()
         tokens_in.wait()
         cot_in.start()
     with jax.named_scope("time_forward"):
@@ -629,17 +631,17 @@
         twins[1].copy(0, unit_t).start()
         attend(merged_t, mixed_t, seqs, biases_t, 4)
         twins[1].copy(2, mixed_t).start()
-        loads[2].wait()
+        loads[3].wait()
         add_residual(x_time, mixed_t, w_to, made, (2, 128))
         pack_time(made, tiles_out)
         first.start()
     with jax.named_scope("first_to_steps"):
         cot_in.wait()
         twins[0].copy(3, g_agent).start()
-        loads[3].wait()
+        loads[4].wait()
         grad_of_mixed(g_agent.at[0:256, :], w_ao, gmix)
         cot_in.drain()
-        loads[4].wait()
+        loads[5].wait()
         first.wait()
         unpack_agent(first_in, x_agent)
     with jax.named_scope("agent_backward"):
@@ -724,11 +726,9 @@
             shape((8, D), F32),
         ],
         in_specs=[
-            pl.BlockSpec(memory_space=pl.ANY),
-            pl.BlockSpec(memory_space=pl.ANY),
-            pl.BlockSpec(memory_space=pltpu.VMEM),
+            pl.BlockSpec(memory_space=pl.ANY)
         ]
-        + [pl.BlockSpec(memory_space=pl.ANY)] * 4,
+        * 7,
         out_specs=[pl.BlockSpec(memory_space=pl.ANY)] + [pl.BlockSpec(memory_space=pltpu.VMEM)] * 4,
         scratch_shapes=[
             pltpu.VMEM((D, 3 * D), BF),
@@ -749,6 +749,7 @@
             pltpu.VMEM((256, D), F32),
             pltpu.VMEM((2, 128, 128), F32),
             pltpu.VMEM((256, 256), F32),
+            pltpu.VMEM((256, STEPS), jnp.int32),
             pltpu.VMEM((2, 512, D), BF),
             pltpu.VMEM((2, 512, 3 * D), BF),
             pltpu.VMEM((2, 512, D), BF),
@@ -759,7 +760,7 @@
         + scatter_bufs()
         + scatter_bufs()
         + [
-            pltpu.SemaphoreType.DMA((5,)),
+            pltpu.SemaphoreType.DMA((6,)),
             pltpu.SemaphoreType.DMA((2,)),
             pltpu.SemaphoreType.DMA((2,)),
             pltpu.SemaphoreType.DMA((3, 16)),

time: 111 us -> 103 us (0.928)
  Pallas kernels: 110 us -> 102 us
    pallas_call x1, Pallas kernels: 108 us -> 99.8 us  [local(): pl.pallas_call(block_kernel, out_shape=[shape((16, 16, D), BF), shape((8,...]
where the time goes in v4:
time: 103 us; the launch traced here: 102 us
  Pallas kernels  102 us (99%)
    pallas_call x1, Pallas kernels, local(): pl.pallas_call(block_kernel, out_shape=[shape((16, 16, D), BF), shape((8,...  99.8 us

profile of v4, /device:TPU:0, one launch (start us, length us, event | category | flops | bytes accessed | tf_op | source)
XLA Modules:
  0.0 102.5 jit_solution(11009128691054022953)
XLA Ops:
  0.6 99.8 %shard_map.110 = (bf16[16,16,1024]{2,1,0:T(8,128)(2,1)}, f32[8,3072]{1,0:T(8,128)}, f32[8,1024]{1,0:T(8,128)}, f32[8,3072]{1,0:T(8,128)}, f32[8,1024]{1,0:T(8,128)}) custom-call(bf16[16,16,1024]{2,1,0:T(8,128)(2,1)} %bitcast.4, bf16[256,1024]{1,0:T(8,128)(2,1)} %bitcast.5, s32[256,128]{1,0:T(8,128)} %bitcast.6, bf16[1024,3072]{1,0:T(8,128)(2,1)} %time_qkv.1, ...), custom_call_target="tpu_custom_call" | custom-call | tf_op jit(solution)/shard_map/pallas_call | solution.py:719
  100.4 2.0 %shard_map.111 = (bf16[16,16,1024]{2,1,0:T(8,128)(2,1)}, f32[8,3072]{1,0:T(8,128)}, f32[8,1024]{1,0:T(8,128)}, f32[8,3072]{1,0:T(8,128)}, f32[8,1024]{1,0:T(8,128)}) custom-call(bf16[16,16,1024]{2,1,0:T(8,128)(2,1)} %get-tuple-element.15.refs_0_, f32[8,3072]{1,0:T(8,128)} %get-tuple-element.16.refs_1_, f32[8,1024]{1,0:T(8,128)} %get-tuple-element.17.refs_2_, ...), custom_call_target="tpu_custom_call" | custom-call | tf_op jit(solution)/shard_map/pallas_call | solution.py:786

commit v5 on v4

--- a/solution.py
+++ b/solution.py
@@ -20,7 +20,7 @@
 NT = (((1,), (1,)), ((), ()))
 TN = (((0,), (0,)), ((), ()))
 
-STREAMS = ((0, 1408, "xyz"), (1408, 2816, "yzx"), (2816, 4096, "zxy"))
+STREAMS = ((0, 1280, "xyz"), (1280, 2816, "yzx"), (2816, 4096, "zxy"))
 
 
 def matmul(left, right, dims=(((1,), (0,)), ((), ()))):
@@ -661,6 +661,9 @@
         for stream in range(3):
             scatters[0].start(stream, ut, ut_mixed, gm_a, g_agent)
     with jax.named_scope("grad_first_to_agents"):
+        for slot, ref in ((0, unit_t), (2, mixed_t)):
+            twins[1].copy(slot, ref).wait_recv()
+        transposed(place, unit_t, mixed_t, ut, ut_mixed, gu)
         back.wait()
         unpack_time(back_in, g_time)
         twins[1].copy_rows(3, g_time).start()
@@ -672,22 +675,20 @@
         for stream in range(3):
             scatters[0].pass_on(stream)
         grad_of_input(x_time, g_own, gm_t, w_tq, gu, made, (2, 128))
+    with jax.named_scope("time_weights"):
+        twins[1].copy(1, gm_t).wait_recv()
+        twins[1].copy_rows(3, g_time).wait_recv()
+        for stream in range(3):
+            scatters[1].start(stream, ut, ut_mixed, gm_t, g_time)
         tokens_out.start()
-        for stream in range(3):
-            scatters[0].second(stream)
-    with jax.named_scope("time_weights"):
-        for slot, ref in enumerate((unit_t, gm_t, mixed_t)):
-            twins[1].copy(slot, ref).wait_recv()
-        twins[1].copy_rows(3, g_time).wait_recv()
-        transposed(place, unit_t, mixed_t, ut, ut_mixed, gu)
-        for stream in range(3):
-            scatters[1].start(stream, ut, ut_mixed, gm_t, g_time)
     with jax.named_scope("rings"):
         outs = ((aq_ref, ao_ref), (tq_ref, to_ref))
         for stream in range(3):
+            scatters[0].second(stream)
+        for stream in range(3):
+            scatters[1].pass_on(stream)
+        for stream in range(3):
             scatters[0].third(stream)
-        for stream in range(3):
-            scatters[1].pass_on(stream)
         for stream in range(3):
             scatters[1].second(stream)
         for stream in range(3):

time: 103 us -> 104 us (level)
  no operation moved by 1% of the time
where the time goes in v5:
time: 104 us; the launch traced here: 103 us
  Pallas kernels  103 us (99%)
    pallas_call x1, Pallas kernels, local(): pl.pallas_call(block_kernel, out_shape=[shape((16, 16, D), BF), shape((8,...  101 us

profile of v5, /device:TPU:0, one launch (start us, length us, event | category | flops | bytes accessed | tf_op | source)
XLA Modules:
  0.0 103.4 jit_solution(8820433124215208604)
XLA Ops:
  0.6 100.8 %shard_map.110 = (bf16[16,16,1024]{2,1,0:T(8,128)(2,1)}, f32[8,3072]{1,0:T(8,128)}, f32[8,1024]{1,0:T(8,128)}, f32[8,3072]{1,0:T(8,128)}, f32[8,1024]{1,0:T(8,128)}) custom-call(bf16[16,16,1024]{2,1,0:T(8,128)(2,1)} %bitcast.4, bf16[256,1024]{1,0:T(8,128)(2,1)} %bitcast.5, s32[256,128]{1,0:T(8,128)} %bitcast.6, bf16[1024,3072]{1,0:T(8,128)(2,1)} %time_qkv.1, ...), custom_call_target="tpu_custom_call" | custom-call | tf_op jit(solution)/shard_map/pallas_call | solution.py:720
  101.4 2.0 %shard_map.111 = (bf16[16,16,1024]{2,1,0:T(8,128)(2,1)}, f32[8,3072]{1,0:T(8,128)}, f32[8,1024]{1,0:T(8,128)}, f32[8,3072]{1,0:T(8,128)}, f32[8,1024]{1,0:T(8,128)}) custom-call(bf16[16,16,1024]{2,1,0:T(8,128)(2,1)} %get-tuple-element.15.refs_0_, f32[8,3072]{1,0:T(8,128)} %get-tuple-element.16.refs_1_, f32[8,1024]{1,0:T(8,128)} %get-tuple-element.17.refs_2_, ...), custom_call_target="tpu_custom_call" | custom-call | tf_op jit(solution)/shard_map/pallas_call | solution.py:787

commit v6 on v5

--- a/solution.py
+++ b/solution.py
@@ -675,20 +675,20 @@
         for stream in range(3):
             scatters[0].pass_on(stream)
         grad_of_input(x_time, g_own, gm_t, w_tq, gu, made, (2, 128))
+        tokens_out.start()
+        for stream in range(3):
+            scatters[0].second(stream)
     with jax.named_scope("time_weights"):
         twins[1].copy(1, gm_t).wait_recv()
         twins[1].copy_rows(3, g_time).wait_recv()
         for stream in range(3):
             scatters[1].start(stream, ut, ut_mixed, gm_t, g_time)
-        tokens_out.start()
     with jax.named_scope("rings"):
         outs = ((aq_ref, ao_ref), (tq_ref, to_ref))
         for stream in range(3):
-            scatters[0].second(stream)
+            scatters[0].third(stream)
         for stream in range(3):
             scatters[1].pass_on(stream)
-        for stream in range(3):
-            scatters[0].third(stream)
         for stream in range(3):
             scatters[1].second(stream)
         for stream in range(3):

time: 104 us -> 102 us (0.981)
    pallas_call x1, Pallas kernels: 101 us -> 99.7 us  [local(): pl.pallas_call(block_kernel, out_shape=[shape((16, 16, D), BF), shape((8,...]
where the time goes in v6:
time: 102 us
  Pallas kernels  102 us (100%)
    pallas_call x1, Pallas kernels, local(): pl.pallas_call(block_kernel, out_shape=[shape((16, 16, D), BF), shape((8,...  99.7 us

profile of v6, /device:TPU:0, one launch (start us, length us, event | category | flops | bytes accessed | tf_op | source)
XLA Modules:
  0.0 102.3 jit_solution(2838767244302002936)
XLA Ops:
  0.6 99.7 %shard_map.110 = (bf16[16,16,1024]{2,1,0:T(8,128)(2,1)}, f32[8,3072]{1,0:T(8,128)}, f32[8,1024]{1,0:T(8,128)}, f32[8,3072]{1,0:T(8,128)}, f32[8,1024]{1,0:T(8,128)}) custom-call(bf16[16,16,1024]{2,1,0:T(8,128)(2,1)} %bitcast.4, bf16[256,1024]{1,0:T(8,128)(2,1)} %bitcast.5, s32[256,128]{1,0:T(8,128)} %bitcast.6, bf16[1024,3072]{1,0:T(8,128)(2,1)} %time_qkv.1, ...), custom_call_target="tpu_custom_call" | custom-call | tf_op jit(solution)/shard_map/pallas_call | solution.py:720
  100.3 2.0 %shard_map.111 = (bf16[16,16,1024]{2,1,0:T(8,128)(2,1)}, f32[8,3072]{1,0:T(8,128)}, f32[8,1024]{1,0:T(8,128)}, f32[8,3072]{1,0:T(8,128)}, f32[8,1024]{1,0:T(8,128)}) custom-call(bf16[16,16,1024]{2,1,0:T(8,128)(2,1)} %get-tuple-element.15.refs_0_, f32[8,3072]{1,0:T(8,128)} %get-tuple-element.16.refs_1_, f32[8,1024]{1,0:T(8,128)} %get-tuple-element.17.refs_2_, ...), custom_call_target="tpu_custom_call" | custom-call | tf_op jit(solution)/shard_map/pallas_call | solution.py:787
